TPU v7x, 512 devices: a whole 4x4x16 slice. The times are simulated.
512 devices in a mesh: pipe: 16 (over z_lo, y), dp: 32 (over z_hi, x, core).
Axes of the slice: x: 4, y: 4, z: 16 (z_hi: 4, z_lo: 4; z = z_hi * 4 + z_lo), core: 2. Of those that a mesh axis runs over, the one named last changes fastest.
Arguments:
- queries: bfloat16 [16, 4096, 4096], P('pipe', 'dp'), may hold values from -6 to 6
- out_grad: bfloat16 [16, 4096, 4096], P('pipe', 'dp'), may hold values from -6 to 6
- keys: bfloat16 [16, 2048, 512], P('pipe', 'dp'), may hold values from -6 to 6
- values: bfloat16 [16, 2048, 512], P('pipe', 'dp'), may hold values from -6 to 6
- kv_weight: bfloat16 [16, 8192, 1024], P('pipe', 'dp'), may hold values from -0.0625 to 0.0625
- stream: bfloat16 [2048, 8192], P(None, 'dp'), may hold values from -640 to 640
- norm_gain: float32 [8192], P('dp'), may hold values from 0.1 to 1.9
- lengths: int32 [32], P('dp'), may hold values from 32 to 128, as said below
Outputs:
- kv_weight_grad: float32 [16, 8192, 1024], P('pipe', 'dp')
- latent_grad: bfloat16 [2048, 8192], P('pipe', 'dp')
- gain_grad: float32 [8192], P('dp')
Inputs may be any that keep to these rules, and one draw needn't show every extreme that they name: `lengths`: each micro-batch has 32 to 128 live tokens; some micro-batch has exactly 128 and another exactly 32.
All inputs are finite; a program needn't handle non-finite values.
Results may differ from a plain program's by a relative error of at most 0.0057.
Values may be sent and summed in bfloat16 or wider, within the bound.
A program may use at most 64 MiB of HBM per device.

v0:
```python
import math
import jax
import jax.numpy as jnp
from jax import lax
from jax.sharding import PartitionSpec as P

D = 8192
HQ = 32
KVH = 4
HD = 128
NORM_EPS = 1e-05


def attention_grads(query_rows, grad_rows, key_rows, value_rows, length):
    token_count = query_rows.shape[0]
    latent_count = key_rows.shape[0]
    group_size = HQ // KVH
    score_scale = 1.0 / math.sqrt(HD)
    token_live = lax.iota(jnp.int32, token_count) < length
    masked = jnp.where(token_live[:, None], grad_rows, jnp.zeros_like(grad_rows))
    query_h = query_rows.reshape(token_count, KVH, group_size, HD)
    grad_h = masked.reshape(token_count, KVH, group_size, HD)
    key_h = key_rows.reshape(latent_count, KVH, HD)
    value_h = value_rows.reshape(latent_count, KVH, HD)
    scores = (
        jnp.einsum("tgqd,jgd->gqjt", query_h, key_h, preferred_element_type=jnp.float32)
        * score_scale
    )
    row_max = jnp.max(scores, axis=2, keepdims=True)
    expo = jnp.exp(scores - row_max)
    prob_values = expo / jnp.sum(expo, axis=2, keepdims=True)
    dprob = jnp.einsum("tgqd,jgd->gqjt", grad_h, value_h, preferred_element_type=jnp.float32)
    centre = jnp.sum(prob_values * dprob, axis=2, keepdims=True)
    dscore = (prob_values * (dprob - centre) * score_scale).astype(jnp.bfloat16)
    probs_b = prob_values.astype(jnp.bfloat16)
    key_grad = jnp.einsum("gqjt,tgqd->jgd", dscore, query_h, preferred_element_type=jnp.float32)
    value_grad = jnp.einsum("gqjt,tgqd->jgd", probs_b, grad_h, preferred_element_type=jnp.float32)
    joined = jnp.concatenate(
        [key_grad.reshape(latent_count, KVH * HD), value_grad.reshape(latent_count, KVH * HD)],
        axis=1,
    )
    return joined.astype(jnp.bfloat16)


def body(queries, out_grad, keys, values, kv_weight, stream, norm_gain, lengths):
    kv_grads = attention_grads(queries[0], out_grad[0], keys[0], values[0], lengths[0])
    promoted = stream.astype(jnp.float32)
    squares = lax.psum(jnp.sum(promoted * promoted, axis=1), "dp")
    inverse = lax.rsqrt(squares / D + NORM_EPS)[:, None]
    normed = promoted * inverse
    latents = (normed * norm_gain[None, :]).astype(jnp.bfloat16)
    gathered = lax.all_gather(kv_grads, "dp", axis=0, tiled=True)
    group_total = lax.axis_size("dp")
    weight = kv_weight[0]
    weight_grad = (
        lax.dot_general(
            latents, gathered, (((0,), (0,)), ((), ())), preferred_element_type=jnp.float32
        )
        / group_total
    )
    row_count = gathered.shape[0] // lax.axis_size("pipe")
    first_row = lax.axis_index("pipe") * row_count
    share_rows = lax.psum_scatter(
        lax.dot_general(
            gathered, weight, (((1,), (1,)), ((), ())), preferred_element_type=jnp.float32
        ),
        "pipe",
        scatter_dimension=0,
        tiled=True,
    )
    normed_share = lax.dynamic_slice_in_dim(normed, first_row, row_count, 0)
    gain_part = jnp.sum(share_rows * normed_share, axis=0)
    gain_grad = lax.psum(gain_part, "pipe") / group_total
    return (weight_grad[None], share_rows.astype(jnp.bfloat16), gain_grad)


def solution(mesh):
    return jax.shard_map(
        body,
        mesh=mesh,
        in_specs=(
            P("pipe", "dp", None),
            P("pipe", "dp", None),
            P("pipe", "dp", None),
            P("pipe", "dp", None),
            P("pipe", "dp", None),
            P(None, "dp"),
            P("dp"),
            P("dp"),
        ),
        out_specs=(P("pipe", "dp", None), P("pipe", "dp"), P("dp")),
        check_vma=False,
    )
```

profile of v0, /device:TPU:128, one launch (start us, length us, event | category | flops | bytes accessed | tf_op | source)
XLA Modules:
  0.0 271.0 jit_solution(11565212643555635086)
XLA Ops:
  7.2 0.0 copy-start
  7.2 0.0 copy-start.3
  7.2 0.0 all-gather.2.cloned.1.call-start
  7.2 1.5 copy.33
  8.7 0.0 copy-done.3
  8.8 0.0 copy-start.2
  8.8 0.5 fusion.9
  9.3 0.0 copy-start.4
  9.3 1.2 fusion.32
  10.5 0.0 copy-done.2
  10.5 1.2 copy.34
  12.4 0.0 copy-done.4
  12.4 2.8 %convolution_bitcast_fusion = f32[4,8,64,128]{3,2,1,0:T(8,128)} fusion(bf16[128,4,8,128]{3,2,1,0:T(8,128)(2,1)} %bitcast.53, pred[128]{0:T(512)(128)(4,1)S(1)} %iota_compare_fusion, bf16[64,4,128,1]{2,1,0,3:T(4,128)(2,1)S(1)} %bitcast.56), kind=kOutput, calls=%fused_computation.13 | convolution fusion | flops 67633152 | bytes 2162816 | tf_op jit(solution)/shard_map/tgqd,jgd->gqjt/dot_general | solution.py:32
  15.2 1.9 fusion.15
  17.2 2.9 %fusion.16 = bf16[4,8,8,128]{3,2,1,0:T(8,128)(2,1)S(1)} fusion(f32[4,8,64,128]{3,2,1,0:T(8,128)} %convolution_bitcast_fusion, bf16[128,4,8,128]{3,2,1,0:T(8,128)(2,1)S(1)} %bitcast.50, f32[4,8,64,128]{3,2,1,0:T(8,128)} %get-tuple-element.6, f32[4,8,128]{2,1,0:T(8,128)S(1)} %get-tuple-element.5), kind=kOutput, calls=%fused_computation.23 | convolution fusion | flops 68980800 | bytes 3227648 | tf_op jit(solution)/shard_map/gqjt,tgqd->jgd/dot_general | solution.py:36
  20.1 0.7 pad_maximum_fusion
  20.8 0.0 all-gather.2.cloned.1.call-update
  20.8 0.0 reduce-scatter.2.cloned.1.call-start
  20.9 94.6 %all-gather.2.cloned.1.call-done = bf16[2048,1024]{1,0:T(8,128)(2,1)} async-done(((bf16[64,1024]{1,0:T(8,128)(2,1)}), bf16[2048,1024]{1,0:T(8,128)(2,1)}) %all-gather.2.cloned.1.call-update) | async-done | bytes 4194320 | tf_op jit(solution)/shard_map/all_gather | solution.py:52
  115.5 0.0 copy-done
  115.5 4.8 %fusion.22 = f32[2048,256]{1,0:T(8,128)} fusion(bf16[2048,1024]{1,0:T(8,128)(2,1)} %all-gather.2.cloned.1.call-done, bf16[1,256,1024]{2,1,0:T(8,128)(2,1)S(1)} %copy-done), kind=kOutput, calls=%fused_computation.30 | convolution fusion | flops 1073741824 | bytes 6815744 | tf_op jit(solution)/shard_map/dot_general | solution.py:64
  120.3 0.0 copy-start.1
  120.3 0.0 reduce-scatter.2.cloned.1.call-update
  120.4 1.2 copy-done.1
  121.6 0.0 copy-start.5
  121.6 0.3 fusion.2
  121.9 91.9 %psum.14 = f32[2048]{0:T(1024)S(1)} all-reduce(f32[2048]{0:T(1024)S(1)} %fusion.2), channel_id=1, replica_groups=mesh['pipe'=16,'dp'=32] {'dp'}, use_global_device_ids=true, to_apply=%region_1.2 | all-reduce | flops 2048 | bytes 16384 | tf_op jit(solution)/shard_map/psum | solution.py:48
  213.8 1.7 convert_multiply_fusion
  215.5 0.0 copy-done.5
  215.5 4.5 %fusion.8 = f32[1,256,1024]{2,1,0:T(8,128)} fusion(bf16[2048,1024]{1,0:T(8,128)(2,1)} %all-gather.2.cloned.1.call-done, f32[256]{0:T(256)S(1)} %copy-done.5, bf16[2048,256]{1,0:T(8,128)(2,1)S(1)} %copy-done.1, f32[2048]{0:T(1024)S(1)} %add_rsqrt_fusion), kind=kOutput, calls=%fused_computation.12 | convolution fusion | flops 1076101120 | bytes 6300672 | tf_op jit(solution)/shard_map/dot_general | solution.py:56
  220.0 0.0 reduce-scatter.2.cloned.1.call-done
  220.0 1.7 multiply_reduce_fusion.1
  221.7 41.9 %psum.15 = f32[256]{0:T(256)S(1)} all-reduce(f32[256]{0:T(256)S(1)} %get-tuple-element.3), channel_id=1, replica_groups=mesh['pipe'=16,'dp'=32] {'pipe'}, use_global_device_ids=true, to_apply=%region_7.8 | all-reduce | flops 256 | bytes 2048 | tf_op jit(solution)/shard_map/psum | solution.py:73
  263.6 0.6 broadcast_multiply_fusion
  (5 shorter events, 0.1 us)
Async XLA Ops:
  7.2 108.4 %copy-start = (bf16[1,256,1024]{2,1,0:T(8,128)(2,1)S(1)}, bf16[1,256,1024]{2,1,0:T(8,128)(2,1)}, u32[]{:S(2)}) copy-start(bf16[1,256,1024]{2,1,0:T(8,128)(2,1)} %param.12) | copy-start | bytes 1572868
  7.2 1.6 copy-start.3
  7.2 108.3 %all-gather.2.cloned.1.call-start = ((), (), s32[]{:S(2)}) async-start(), calls=%async_computation.1 | async-start | bytes 4325376 | tf_op jit(solution)/shard_map/all_gather | solution.py:52
  8.8 1.7 copy-start.2
  9.3 3.1 %copy-start.4 = (bf16[1,64,512]{2,1,0:T(8,128)(2,1)S(1)}, bf16[1,64,512]{2,1,0:T(8,128)(2,1)}, u32[]{:S(2)}) copy-start(bf16[1,64,512]{2,1,0:T(8,128)(2,1)} %param.11) | copy-start | bytes 196612
  20.8 199.2 %reduce-scatter.2.cloned.1.call-start = ((), (), s32[]{:S(2)}) async-start(), calls=%async_computation.2 | async-start | bytes 2228224 | tf_op jit(solution)/shard_map/reduce_scatter | solution.py:63
  120.3 1.2 copy-start.1
  121.6 93.9 %copy-start.5 = (f32[256]{0:T(256)S(1)}, f32[256]{0:T(256)}, u32[]{:S(2)}) copy-start(f32[256]{0:T(256)} %param.14) | copy-start | bytes 3076
Sparse Core Ops, SparseCore 0:
  20.9 94.5 all-gather.1
  120.5 92.4 reduce-scatter.1
where the time goes:
time: 271 us
  blocking collectives  134 us (49%)
  waiting for transfers between devices  94.7 us (35%)
  matrix products  17.6 us (6%)
  between operations  14.8 us (5%)
  other arithmetic  6.15 us (2%)
  local copies, waits for them, and re-layouts  3.97 us (1%)
    all_gather x1, waiting for transfers between devices, body(): gathered = lax.all_gather(kv_grads, 'dp', axis=0, tiled=True)  94.6 us
    psum x1, blocking collectives, body(): squares = lax.psum(jnp.sum(promoted * promoted, axis=1), 'dp')  91.9 us
    psum x1, blocking collectives, body(): gain_grad = lax.psum(gain_part, 'pipe') / group_total  41.9 us
  transfers between devices with their start and end apart: 2, of which 1 were waited for; matrix products, arithmetic and copies ran while one was open for 2% of the time, Pallas kernels for 0%

commit v1 on v0

--- a/solution.py
+++ b/solution.py
@@ -49,7 +49,9 @@
     inverse = lax.rsqrt(squares / D + NORM_EPS)[:, None]
     normed = promoted * inverse
     latents = (normed * norm_gain[None, :]).astype(jnp.bfloat16)
-    gathered = lax.all_gather(kv_grads, "dp", axis=0, tiled=True)
+    gathered = jnp.concatenate(
+        lax.all_to_all(jnp.stack([kv_grads] * lax.axis_size("dp")), "dp", 0, 0), axis=0
+    )
     group_total = lax.axis_size("dp")
     weight = kv_weight[0]
     weight_grad = (

time: 271 us -> 377 us (1.39)
  the two profiles are of different devices: /device:TPU:128 before, /device:TPU:16 now
where the time goes in v1:
time: 377 us
  blocking collectives  335 us (89%)
  matrix products  15.5 us (4%)
  between operations  14.8 us (4%)
  local copies, waits for them, and re-layouts  6.42 us (2%)
  other arithmetic  5.49 us (1%)
    all_to_all x1, blocking collectives, body(): lax.all_to_all(jnp.stack([kv_grads] * lax.axis_size('dp')), 'dp', 0, 0)  206 us
    psum x1, blocking collectives, body(): squares = lax.psum(jnp.sum(promoted * promoted, axis=1), 'dp')  89.8 us
    psum x1, blocking collectives, body(): gain_grad = lax.psum(gain_part, 'pipe') / group_total  39.1 us
  transfers between devices with their start and end apart: 1, of which 0 were waited for; matrix products, arithmetic and copies ran while one was open for 2% of the time, Pallas kernels for 0%

profile of v1, /device:TPU:16, one launch (start us, length us, event | category | flops | bytes accessed | tf_op | source)
XLA Modules:
  0.0 377.0 jit_solution(7771388425850751327)
XLA Ops:
  7.2 0.0 copy-start
  7.2 0.0 copy-start.4
  7.2 0.0 reduce-scatter.2.cloned.1.call-start
  7.2 1.5 copy.33
  8.7 0.0 copy-done.4
  8.8 0.0 copy-start.3
  8.8 0.5 fusion.9
  9.3 0.0 copy-start.5
  9.3 1.2 fusion.32
  10.5 0.0 copy-done.3
  10.5 1.2 copy.34
  12.4 0.0 copy-done.5
  12.4 2.8 convolution_bitcast_fusion
  15.3 1.9 fusion.15
  17.2 2.9 fusion.16
  20.2 0.5 stack.2
  20.7 205.9 %all_to_all.5 = bf16[32,64,1024]{2,1,0:T(8,128)(2,1)S(1)} all-to-all(bf16[32,64,1024]{2,1,0:T(8,128)(2,1)S(1)} %stack.2), channel_id=1, replica_groups=mesh['pipe'=16,'dp'=32] {'dp'}, dimensions={0} | all-to-all | bytes 8388608 | tf_op jit(solution)/shard_map/all_to_all | solution.py:53
  226.6 0.0 copy-start.2
  226.6 1.9 copy-done.2
  228.5 0.0 copy-done
  228.5 2.7 fusion.22
  231.3 0.0 copy-start.1
  231.3 0.0 reduce-scatter.2.cloned.1.call-update
  231.3 1.2 copy-done.1
  232.5 0.0 copy-start.6
  232.5 0.3 fusion.2
  232.8 89.8 %psum.14 = f32[2048]{0:T(1024)S(1)} all-reduce(f32[2048]{0:T(1024)S(1)} %fusion.2), channel_id=1, replica_groups=mesh['pipe'=16,'dp'=32] {'dp'}, use_global_device_ids=true, to_apply=%region_1.2 | all-reduce | flops 2048 | bytes 16384 | tf_op jit(solution)/shard_map/psum | solution.py:48
  322.6 1.7 convert_multiply_fusion
  324.3 0.0 copy-done.6
  324.3 4.5 %fusion.8 = f32[1,256,1024]{2,1,0:T(8,128)} fusion(bf16[2048,1024]{1,0:T(8,128)(2,1)} %bitcast.51, f32[256]{0:T(256)S(1)} %copy-done.6, bf16[2048,256]{1,0:T(8,128)(2,1)S(1)} %copy-done.1, f32[2048]{0:T(1024)S(1)} %add_rsqrt_fusion), kind=kOutput, calls=%fused_computation.12 | convolution fusion | flops 1076101120 | bytes 6300672 | tf_op jit(solution)/shard_map/dot_general | solution.py:58
  328.8 0.0 reduce-scatter.2.cloned.1.call-done
  328.8 1.7 multiply_reduce_fusion.1
  330.5 39.1 %psum.15 = f32[256]{0:T(256)S(1)} all-reduce(f32[256]{0:T(256)S(1)} %get-tuple-element.3), channel_id=1, replica_groups=mesh['pipe'=16,'dp'=32] {'pipe'}, use_global_device_ids=true, to_apply=%region_7.8 | all-reduce | flops 256 | bytes 2048 | tf_op jit(solution)/shard_map/psum | solution.py:75
  369.6 0.6 broadcast_multiply_fusion
  (6 shorter events, 0.1 us)
Async XLA Ops:
  7.2 221.4 %copy-start = (bf16[1,256,1024]{2,1,0:T(8,128)(2,1)S(1)}, bf16[1,256,1024]{2,1,0:T(8,128)(2,1)}, u32[]{:S(2)}) copy-start(bf16[1,256,1024]{2,1,0:T(8,128)(2,1)} %param.12) | copy-start | bytes 1572868
  7.2 1.6 copy-start.4
  7.2 321.7 %reduce-scatter.2.cloned.1.call-start = ((), (), s32[]{:S(2)}) async-start(), calls=%async_computation.2 | async-start | bytes 2228224 | tf_op jit(solution)/shard_map/reduce_scatter | solution.py:65
  8.8 1.7 copy-start.3
  9.3 3.1 copy-start.5
  226.6 1.9 copy-start.2
  231.3 1.2 copy-start.1
  232.5 91.8 %copy-start.6 = (f32[256]{0:T(256)S(1)}, f32[256]{0:T(256)}, u32[]{:S(2)}) copy-start(f32[256]{0:T(256)} %param.14) | copy-start | bytes 3076
Sparse Core Ops, SparseCore 0:
  231.4 83.3 reduce-scatter.1
